TPU v7x, 32 devices: a whole 2x2x4 slice. The times are simulated.
32 devices in a mesh: seq: 4 (over x, core), batch: 8 (over z, y).
Axes of the slice: x: 2, y: 2, z: 4, core: 2. Of those that a mesh axis runs over, the one named last changes fastest.
Arguments:
- tokens: bfloat16 [8, 1024, 1024], P('batch', 'seq'), may hold values from -6 to 6
- w_query: bfloat16 [1024, 1024], P(('seq', 'batch')), may hold values from -0.25 to 0.25
- w_key: bfloat16 [1024, 1024], P(('seq', 'batch')), may hold values from -0.25 to 0.25
- w_value: bfloat16 [1024, 1024], P(('seq', 'batch')), may hold values from -0.1875 to 0.1875
- w_out: bfloat16 [1024, 1024], P(('seq', 'batch')), may hold values from -0.375 to 0.375
- gain_attn: bfloat16 [1024], P(('seq', 'batch')), may hold values from 0.25 to 1.75
- w_gate: bfloat16 [1024, 4096], P(('seq', 'batch')), may hold values from -0.1875 to 0.1875
- w_up: bfloat16 [1024, 4096], P(('seq', 'batch')), may hold values from -0.1875 to 0.1875
- w_down: bfloat16 [4096, 1024], P(('seq', 'batch')), may hold values from -0.125 to 0.125
- gain_ffn: bfloat16 [1024], P(('seq', 'batch')), may hold values from 0.25 to 1.75
- counts: int32 [8, 4], P('batch'), may hold values from 0 to 256, as said below
- cotangent: bfloat16 [8, 1024, 1024], P('batch', 'seq'), may hold values from -6 to 6
Outputs:
- block_output: bfloat16 [8, 1024, 1024], P('batch', 'seq')
- input_grad: float32 [8, 1024, 1024], P('batch', 'seq')
- grad_w_query: float32 [1024, 1024], P(('seq', 'batch'))
- grad_w_key: float32 [1024, 1024], P(('seq', 'batch'))
- grad_w_value: float32 [1024, 1024], P(('seq', 'batch'))
- grad_w_out: float32 [1024, 1024], P(('seq', 'batch'))
- grad_gain_attn: float32 [1024], P(('seq', 'batch'))
- grad_w_gate: float32 [1024, 4096], P(('seq', 'batch'))
- grad_w_up: float32 [1024, 4096], P(('seq', 'batch'))
- grad_w_down: float32 [4096, 1024], P(('seq', 'batch'))
- grad_gain_ffn: float32 [1024], P(('seq', 'batch'))
Inputs may be any that keep to these rules, and one draw needn't show every extreme that they name: counts[s, i] = min(max(L_s - i * 256, 0), 256) for a length L_s of sequence s between 256 and 1024; some sequence has length 1024 and another length 256.
All inputs are finite; a program needn't handle non-finite values.
Results may differ from a plain program's by a relative error of at most 0.017.
Values may be sent and summed in bfloat16 or wider, within the bound.
No kernel may reach another device: no remote copies, remote signals or barrier semaphores. Data moves between devices by JAX's collectives and lax.ppermute only.
A program may use at most 192 MiB of HBM per device.

v0:
```python
import math
import jax
import jax.numpy as jnp
from jax import lax
from jax.sharding import PartitionSpec as P

HEADS = 16
EPSILON = 1e-05


def rms_scale(source):
    return lax.rsqrt(jnp.mean(source * source, axis=-1, keepdims=True) + EPSILON)


def norm_back(incoming, source, gain_full):
    inverse = rms_scale(source)
    scaled = incoming * gain_full
    grad_source = inverse * (
        scaled - source * (inverse * inverse) * jnp.mean(scaled * source, axis=-1, keepdims=True)
    )
    grad_gain = jnp.sum(incoming * source * inverse, axis=0)
    return (grad_source, grad_gain)


def project(left, right):
    return jnp.dot(left, right, preferred_element_type=jnp.float32)


def project_back(grad_rows, weight):
    return jnp.einsum("td,ed->te", grad_rows, weight, preferred_element_type=jnp.float32)


def weight_grad(left, grad_rows):
    return jnp.einsum("td,te->de", left, grad_rows, preferred_element_type=jnp.float32)


def column_grad(left, grad_rows):
    return weight_grad(left, grad_rows)


def local(
    tokens,
    w_query,
    w_key,
    w_value,
    w_out,
    gain_attn,
    w_gate,
    w_up,
    w_down,
    gain_ffn,
    counts,
    cotangent,
):
    source = tokens[0].astype(jnp.float32)
    row_count, model_width = source.shape
    head_count = HEADS
    head_width = model_width // head_count
    shard_count = lax.axis_size("seq")
    shard_index = lax.axis_index("seq")
    seq_length = row_count * shard_count
    score_scale = head_width ** (-0.5)
    score_offset = -math.log(seq_length)
    count_row = counts[0]
    query_first = shard_index * row_count
    query_last = query_first + row_count - 1
    query_pos = query_first + jnp.arange(row_count, dtype=jnp.int32)
    shard_ids = jnp.arange(shard_count, dtype=jnp.int32)

    def split_heads(matrix):
        return matrix.reshape(matrix.shape[0], head_count, head_width)

    def gating(query_heads, key_block):
        key_rows = key_block.shape[0]
        logits = (
            jnp.einsum(
                "qhe,khe->hqk",
                query_heads,
                split_heads(key_block),
                preferred_element_type=jnp.float32,
            )
            * score_scale
            + score_offset
        )
        key_pos = jnp.arange(key_rows, dtype=jnp.int32)
        owner = key_pos // row_count
        place = key_pos - owner * row_count
        valid_count = jnp.sum(
            jnp.where(owner[:, None] == shard_ids[None, :], count_row[None, :], 0), axis=1
        )
        allowed = (place < valid_count)[None, :] & (key_pos[None, :] <= query_pos[:, None])
        return (jax.nn.sigmoid(logits), allowed[None])

    def unchanged(carry):
        return carry

    attn_full = (
        lax.all_gather(w_query, ("seq", "batch"), axis=0, tiled=True),
        lax.all_gather(w_key, ("seq", "batch"), axis=0, tiled=True),
        lax.all_gather(w_value, ("seq", "batch"), axis=0, tiled=True),
        lax.all_gather(w_out, ("seq", "batch"), axis=0, tiled=True),
        lax.all_gather(gain_attn, ("seq", "batch"), axis=0, tiled=True),
    )
    gain_one = attn_full[4].astype(jnp.float32)
    normed_attn = (source * rms_scale(source) * gain_one).astype(jnp.bfloat16)
    query = project(normed_attn, attn_full[0]).astype(jnp.bfloat16)
    key_rows_mine = project(normed_attn, attn_full[1]).astype(jnp.bfloat16)
    value_rows_mine = project(normed_attn, attn_full[2]).astype(jnp.bfloat16)
    query_heads = split_heads(query)
    key_block = lax.all_gather(key_rows_mine, "seq", axis=0, tiled=True)
    value_block = lax.all_gather(value_rows_mine, "seq", axis=0, tiled=True)

    def attend_compute(summed):
        gates, allowed = gating(query_heads, key_block)
        probs = jnp.where(allowed, gates, 0.0).astype(jnp.bfloat16)
        mixed = jnp.einsum(
            "hqk,khe->qhe", probs, split_heads(value_block), preferred_element_type=jnp.float32
        )
        return mixed.reshape(row_count, model_width)

    attended_sum = lax.cond(
        jnp.int32(0) <= query_last,
        attend_compute,
        unchanged,
        jnp.zeros((row_count, model_width), jnp.float32),
    )
    attended = attended_sum.astype(jnp.bfloat16)
    resid = source + project(attended, attn_full[3])
    ffn_full = (
        lax.all_gather(w_gate, ("seq", "batch"), axis=0, tiled=True),
        lax.all_gather(w_up, ("seq", "batch"), axis=0, tiled=True),
        lax.all_gather(w_down, ("seq", "batch"), axis=0, tiled=True),
        lax.all_gather(gain_ffn, ("seq", "batch"), axis=0, tiled=True),
    )
    gain_two = ffn_full[3].astype(jnp.float32)
    normed_ffn = (resid * rms_scale(resid) * gain_two).astype(jnp.bfloat16)
    gate = project(normed_ffn, ffn_full[0])
    up_proj = project(normed_ffn, ffn_full[1])
    gate_sigma = jax.nn.sigmoid(gate)
    hidden = (gate * gate_sigma * up_proj).astype(jnp.bfloat16)
    block_output = (resid + project(hidden, ffn_full[2])).astype(jnp.bfloat16)
    ffn_back = (
        lax.all_gather(w_gate, ("seq", "batch"), axis=0, tiled=True),
        lax.all_gather(w_up, ("seq", "batch"), axis=0, tiled=True),
        lax.all_gather(w_down, ("seq", "batch"), axis=0, tiled=True),
        lax.all_gather(gain_ffn, ("seq", "batch"), axis=0, tiled=True),
    )
    cot_rows = cotangent[0]
    grad_hidden = project_back(cot_rows, ffn_back[2])
    grad_gate = (
        grad_hidden * up_proj * (gate_sigma + gate * gate_sigma * (1.0 - gate_sigma))
    ).astype(jnp.bfloat16)
    grad_up = (grad_hidden * gate * gate_sigma).astype(jnp.bfloat16)
    grad_normed_ffn = project_back(grad_gate, ffn_back[0]) + project_back(grad_up, ffn_back[1])
    grad_norm_two, grad_gain_ffn = norm_back(grad_normed_ffn, resid, gain_two)
    grad_resid = cot_rows.astype(jnp.float32) + grad_norm_two
    grad_w_gate = lax.psum_scatter(
        column_grad(normed_ffn, grad_gate), ("seq", "batch"), scatter_dimension=0, tiled=True
    )
    grad_w_up = lax.psum_scatter(
        column_grad(normed_ffn, grad_up), ("seq", "batch"), scatter_dimension=0, tiled=True
    )
    grad_w_down = lax.psum_scatter(
        column_grad(hidden, cot_rows), ("seq", "batch"), scatter_dimension=0, tiled=True
    )
    attn_back = (
        lax.all_gather(w_query, ("seq", "batch"), axis=0, tiled=True),
        lax.all_gather(w_key, ("seq", "batch"), axis=0, tiled=True),
        lax.all_gather(w_value, ("seq", "batch"), axis=0, tiled=True),
        lax.all_gather(w_out, ("seq", "batch"), axis=0, tiled=True),
        lax.all_gather(gain_attn, ("seq", "batch"), axis=0, tiled=True),
    )
    resid_low = grad_resid.astype(jnp.bfloat16)
    grad_attended = project_back(resid_low, attn_back[3]).astype(jnp.bfloat16)
    grad_heads = split_heads(grad_attended)
    start_state = (
        jnp.zeros((row_count, model_width), jnp.float32),
        jnp.zeros((seq_length, model_width), jnp.float32),
        jnp.zeros((seq_length, model_width), jnp.float32),
    )
    reverse_key_block = lax.all_gather(key_rows_mine, "seq", axis=0, tiled=True)
    reverse_value_block = lax.all_gather(value_rows_mine, "seq", axis=0, tiled=True)

    def reverse_compute(summed):
        key_rows = reverse_key_block.shape[0]
        key_heads = split_heads(reverse_key_block)
        gates, allowed = gating(query_heads, reverse_key_block)
        probs = jnp.where(allowed, gates, 0.0).astype(jnp.bfloat16)
        value_term = jnp.einsum(
            "hqk,qhe->khe", probs, grad_heads, preferred_element_type=jnp.float32
        ).reshape(key_rows, model_width)
        grad_probs = jnp.einsum(
            "qhe,khe->hqk",
            grad_heads,
            split_heads(reverse_value_block),
            preferred_element_type=jnp.float32,
        )
        grad_scores = jnp.where(allowed, grad_probs * gates * (1.0 - gates), 0.0).astype(
            jnp.bfloat16
        )
        query_term = (
            jnp.einsum("hqk,khe->qhe", grad_scores, key_heads, preferred_element_type=jnp.float32)
            * score_scale
        )
        key_term = (
            jnp.einsum("hqk,qhe->khe", grad_scores, query_heads, preferred_element_type=jnp.float32)
            * score_scale
        ).reshape(key_rows, model_width)
        grad_query_sum = query_term.reshape(row_count, model_width)
        return (grad_query_sum, key_term, value_term)

    grad_query_sum, grad_key_full, grad_value_full = lax.cond(
        jnp.int32(0) <= query_last, reverse_compute, unchanged, start_state
    )
    grad_key_mine, grad_value_mine = (
        lax.psum_scatter(
            grad_key_full.astype(jnp.bfloat16), "seq", scatter_dimension=0, tiled=True
        ).astype(jnp.float32),
        lax.psum_scatter(
            grad_value_full.astype(jnp.bfloat16), "seq", scatter_dimension=0, tiled=True
        ).astype(jnp.float32),
    )
    grad_query = grad_query_sum.astype(jnp.bfloat16)
    grad_key = grad_key_mine.astype(jnp.bfloat16)
    grad_value = grad_value_mine.astype(jnp.bfloat16)
    grad_normed_attn = (
        project_back(grad_query, attn_back[0])
        + project_back(grad_key, attn_back[1])
        + project_back(grad_value, attn_back[2])
    )
    grad_norm_one, grad_gain_attn = norm_back(grad_normed_attn, source, gain_one)
    input_grad = grad_resid + grad_norm_one
    projected_grads = jnp.concatenate([grad_query, grad_key, grad_value], axis=1)
    attn_grads = lax.psum_scatter(
        jnp.concatenate(
            [column_grad(normed_attn, projected_grads), column_grad(attended, resid_low)], axis=1
        ),
        ("seq", "batch"),
        scatter_dimension=0,
        tiled=True,
    )
    gain_attn_mine, gain_ffn_mine = (
        lax.psum_scatter(grad_gain_attn, ("seq", "batch"), scatter_dimension=0, tiled=True),
        lax.psum_scatter(grad_gain_ffn, ("seq", "batch"), scatter_dimension=0, tiled=True),
    )
    grad_w_query = attn_grads[:, :model_width]
    grad_w_key = attn_grads[:, model_width : 2 * model_width]
    grad_w_value = attn_grads[:, 2 * model_width : 3 * model_width]
    grad_w_out = attn_grads[:, 3 * model_width :]
    return (
        block_output[None],
        input_grad[None],
        grad_w_query,
        grad_w_key,
        grad_w_value,
        grad_w_out,
        gain_attn_mine,
        grad_w_gate,
        grad_w_up,
        grad_w_down,
        gain_ffn_mine,
    )


def solution(mesh):
    in_specs = (
        P("batch", "seq", None),
        P(("seq", "batch"), None),
        P(("seq", "batch"), None),
        P(("seq", "batch"), None),
        P(("seq", "batch"), None),
        P(("seq", "batch")),
        P(("seq", "batch"), None),
        P(("seq", "batch"), None),
        P(("seq", "batch"), None),
        P(("seq", "batch")),
        P("batch", None),
        P("batch", "seq", None),
    )
    out_specs = (
        P("batch", "seq", None),
        P("batch", "seq", None),
        P(("seq", "batch"), None),
        P(("seq", "batch"), None),
        P(("seq", "batch"), None),
        P(("seq", "batch"), None),
        P(("seq", "batch")),
        P(("seq", "batch"), None),
        P(("seq", "batch"), None),
        P(("seq", "batch"), None),
        P(("seq", "batch")),
    )
    return jax.shard_map(local, mesh=mesh, in_specs=in_specs, out_specs=out_specs, check_vma=False)
```

profile of v0, /device:TPU:0, one launch (start us, length us, event | category | flops | bytes accessed | tf_op | source)
XLA Modules:
  0.0 2127.6 jit_solution(17704540515414183479)
XLA Ops:
  7.2 0.7 all-gather.10.cloned.1.call-update
  8.0 0.7 all-gather.16.cloned.1.call-update
  8.7 0.7 all-gather.14.cloned.1.call-update
  9.5 0.8 dynamic-update-slice
  10.3 0.8 dynamic-update-slice.1
  11.2 42.1 %all-reduce.5 = (bf16[1024]{0:T(1024)(128)(2,1)S(1)}, bf16[1024]{0:T(1024)(128)(2,1)S(1)}) all-reduce(bf16[1024]{0:T(1024)(128)(2,1)S(1)} %dynamic-update-slice, bf16[1024]{0:T(1024)(128)(2,1)S(1)} %dynamic-update-slice.1), channel_id=1, replica_groups=mesh['seq'=4,'batch'=8] {'seq','batch'}, use_global_device_ids=true, to_apply=%add | all-reduce | flops 2048 | bytes 8192
  53.2 1.2 fusion.30
  55.0 15.1 all-gather.10.cloned.1.call-done
  70.1 3.3 convolution_convert_fusion.3
  73.5 54.8 %all-gather.16.cloned.1.call-done = bf16[1024,1024]{1,0:T(8,128)(2,1)} async-done(((bf16[32,1024]{1,0:T(8,128)(2,1)}), bf16[1024,1024]{1,0:T(8,128)(2,1)}) %all-gather.16.cloned.1.call-update) | async-done | bytes 2097168 | tf_op jit(solution)/shard_map/all_gather | solution.py:100
  128.3 3.1 convolution_convert_fusion.1
  132.1 0.7 all-gather.22.cloned.1.call-update
  132.9 0.7 all-gather.24.cloned.1.call-update
  134.4 52.2 %all-gather.14.cloned.1.call-done = bf16[1024,1024]{1,0:T(8,128)(2,1)} async-done(((bf16[32,1024]{1,0:T(8,128)(2,1)}), bf16[1024,1024]{1,0:T(8,128)(2,1)}) %all-gather.14.cloned.1.call-update) | async-done | bytes 2097168 | tf_op jit(solution)/shard_map/all_gather | solution.py:98
  186.5 2.3 convolution_convert_fusion.2
  188.9 1.0 copy.44
  189.9 20.1 all-gather.12.cloned.1.call-done
  210.0 24.6 %all-gather.18.cloned.1.call-done = bf16[1024,1024]{1,0:T(8,128)(2,1)} async-done(((bf16[256,1024]{1,0:T(8,128)(2,1)}), bf16[1024,1024]{1,0:T(8,128)(2,1)}) %all-gather.18.cloned.1.call-update) | async-done | bytes 2097168 | tf_op jit(solution)/shard_map/all_gather | solution.py:111
  234.6 16.6 conditional.2
  234.6 4.2 copy.46
  238.8 2.5 copy.45
  241.7 9.5 fusion.1
  251.2 42.6 %all-gather.20.cloned.1.call-done = bf16[1024,1024]{1,0:T(8,128)(2,1)} async-done(((bf16[32,1024]{1,0:T(8,128)(2,1)}), bf16[1024,1024]{1,0:T(8,128)(2,1)}) %all-gather.20.cloned.1.call-update) | async-done | bytes 2097168 | tf_op jit(solution)/shard_map/all_gather | solution.py:101
  293.8 2.4 multiply_reduce_fusion.2
  296.4 76.3 %all-gather.22.cloned.1.call-done = bf16[1024,4096]{1,0:T(8,128)(2,1)} async-done(((bf16[32,4096]{1,0:T(8,128)(2,1)}), bf16[1024,4096]{1,0:T(8,128)(2,1)}) %all-gather.22.cloned.1.call-update) | async-done | bytes 8388624 | tf_op jit(solution)/shard_map/all_gather | solution.py:130
  372.7 7.7 fusion.56
  380.4 71.0 %all-gather.24.cloned.1.call-done = bf16[1024,4096]{1,0:T(8,128)(2,1)} async-done(((bf16[32,4096]{1,0:T(8,128)(2,1)}), bf16[1024,4096]{1,0:T(8,128)(2,1)}) %all-gather.24.cloned.1.call-update) | async-done | bytes 8388624 | tf_op jit(solution)/shard_map/all_gather | solution.py:131
  451.5 7.7 fusion.57
  459.2 71.0 %all-gather.26.cloned.1.call-done = bf16[4096,1024]{1,0:T(8,128)(2,1)} async-done(((bf16[128,1024]{1,0:T(8,128)(2,1)}), bf16[4096,1024]{1,0:T(8,128)(2,1)}) %all-gather.26.cloned.1.call-update) | async-done | bytes 8388624 | tf_op jit(solution)/shard_map/all_gather | solution.py:132
  530.2 12.5 multiply_convert_fusion
  542.7 7.3 fusion.58
  550.0 2.6 multiply_reduce_fusion
  553.0 1.5 convolution_convert_fusion
  554.6 52.7 %conditional.3 = (bf16[1024,1024]{0,1:T(8,128)(2,1)}, bf16[1024,1024]{0,1:T(8,128)(2,1)}, bf16[256,1024]{0,1:T(8,128)(2,1)}) conditional(s32[]{:T(128)} %convert_element_type.97, () %tuple.28, (s32[4]{0:T(128)S(1)}, s32[1,4]{1,0:T(1,128)S(1)}, s32[256]{0:T(256)S(1)}, bf16[256,1024]{1,0:T(8,128)(2,1)}, bf16[1024,1024]{1,0:T(8,128)(2,1)}, ...), branch_computations={%region_6.7_spmd, %region_7.9_spmd} | conditional | flops 2733668352 | bytes 136596672 | solution.py:212
  554.6 4.0 copy.49
  558.6 9.6 add_divide_fusion
  568.1 2.0 copy.47
  570.2 4.3 copy.48
  574.9 13.4 select_convert_fusion.2
  588.3 6.5 convolution_multiply_fusion
  594.8 8.9 fusion.11
  603.7 3.6 fusion.14
  607.4 0.7 reduce-scatter.9.cloned.1.call-update
  608.1 3.7 fusion.45
  611.8 25.4 %reduce-scatter.7.cloned.1.call-done = bf16[256,1024]{0,1:T(8,128)(2,1)} async-done(((bf16[1024,1024]{0,1:T(8,128)(2,1)}), bf16[256,1024]{0,1:T(8,128)(2,1)}) %reduce-scatter.7.cloned.1.call-update) | async-done | bytes 524304 | tf_op jit(solution)/shard_map/reduce_scatter | solution.py:216
  637.3 33.7 %reduce-scatter.9.cloned.1.call-done = bf16[256,1024]{0,1:T(8,128)(2,1)} async-done(((bf16[1024,1024]{0,1:T(8,128)(2,1)}), bf16[256,1024]{0,1:T(8,128)(2,1)}) %reduce-scatter.9.cloned.1.call-update) | async-done | bytes 524304 | tf_op jit(solution)/shard_map/reduce_scatter | solution.py:219
  671.0 3.5 fusion.22
  674.5 6.1 pad_maximum_fusion
  680.8 9.9 fusion.60
  690.8 9.7 fusion.61
  700.6 1.0 copy-done.14
  701.6 9.7 fusion.41
  711.3 2.5 fusion.59
  713.9 7.3 fusion.29
  721.2 0.8 convolution_add_fusion.1
  722.3 0.8 copy-done.10
  723.0 1.1 fusion.40
  724.1 46.5 %all-reduce.4 = (f32[1024]{0:T(1024)S(1)}, f32[1024]{0:T(1024)S(1)}) all-reduce(f32[1024]{0:T(1024)S(1)} %get-tuple-element.116, f32[1024]{0:T(1024)S(1)} %get-tuple-element.114), channel_id=5, replica_groups=mesh['seq'=4,'batch'=8] {'seq','batch'}, use_global_device_ids=true, to_apply=%region_14.15.clone | all-reduce | flops 2048 | bytes 16384
  771.8 1.3 fusion.37
  773.1 267.3 %reduce-scatter.11.cloned.1.call-done = f32[32,4096]{1,0:T(8,128)} async-done(((f32[1024,4096]{1,0:T(8,128)}), f32[32,4096]{1,0:T(8,128)}) %reduce-scatter.11.cloned.1.call-update) | async-done | bytes 524304 | tf_op jit(solution)/shard_map/reduce_scatter | solution.py:234
  1040.4 1.9 fusion.55
  1042.3 358.3 %reduce-scatter.13.cloned.1.call-done = f32[32,4096]{1,0:T(8,128)} async-done(((f32[1024,4096]{1,0:T(8,128)}), f32[32,4096]{1,0:T(8,128)}) %reduce-scatter.13.cloned.1.call-update) | async-done | bytes 524304 | tf_op jit(solution)/shard_map/reduce_scatter | solution.py:157
  1400.6 360.1 %reduce-scatter.15.cloned.1.call-done = f32[32,4096]{1,0:T(8,128)} async-done(((f32[1024,4096]{1,0:T(8,128)}), f32[32,4096]{1,0:T(8,128)}) %reduce-scatter.15.cloned.1.call-update) | async-done | bytes 524304 | tf_op jit(solution)/shard_map/reduce_scatter | solution.py:160
  1760.7 360.1 %reduce-scatter.17.cloned.1.call-done = f32[128,1024]{1,0:T(8,128)} async-done(((f32[4096,1024]{1,0:T(8,128)}), f32[128,1024]{1,0:T(8,128)}) %reduce-scatter.17.cloned.1.call-update) | async-done | bytes 524304 | tf_op jit(solution)/shard_map/reduce_scatter | solution.py:163
  (90 shorter events, 5.4 us)
Async XLA Ops:
  7.2 121.1 %copy-start.1 = (bf16[1,256,1024]{2,1,0:T(8,128)(2,1)S(1)}, bf16[1,256,1024]{2,1,0:T(8,128)(2,1)}, u32[]{:S(2)}) copy-start(bf16[1,256,1024]{2,1,0:T(8,128)(2,1)} %param.16) | copy-start | bytes 1572868
  7.2 62.9 %all-gather.10.cloned.1.call-start = ((), (), s32[]{:S(2)}) async-start(), calls=%async_computation.6 | async-start | bytes 2162688 | tf_op jit(solution)/shard_map/all_gather | solution.py:99
  7.9 120.4 %all-gather.16.cloned.1.call-start = ((), (), s32[]{:S(2)}) async-start(), calls=%async_computation.9 | async-start | bytes 2162688 | tf_op jit(solution)/shard_map/all_gather | solution.py:100
  8.7 177.9 %all-gather.14.cloned.1.call-start = ((), (), s32[]{:S(2)}) async-start(), calls=%async_computation.8 | async-start | bytes 2162688 | tf_op jit(solution)/shard_map/all_gather | solution.py:98
  9.4 200.6 %all-gather.12.cloned.1.call-start = ((), (), s32[]{:S(2)}) async-start(), calls=%async_computation.7 | async-start | bytes 2621440 | tf_op jit(solution)/shard_map/all_gather | solution.py:110
  73.4 161.1 %copy-start.18 = (s32[1,4]{1,0:T(1,128)S(1)}, s32[1,4]{1,0:T(1,128)}, u32[]{:S(2)}) copy-start(s32[1,4]{1,0:T(1,128)} %param.26) | copy-start | bytes 52
  73.5 161.1 %all-gather.18.cloned.1.call-start = ((), (), s32[]{:S(2)}) async-start(), calls=%async_computation.10 | async-start | bytes 2621440 | tf_op jit(solution)/shard_map/all_gather | solution.py:111
  131.5 162.3 %all-gather.20.cloned.1.call-start = ((), (), s32[]{:S(2)}) async-start(), calls=%async_computation.11 | async-start | bytes 2162688 | tf_op jit(solution)/shard_map/all_gather | solution.py:101
  132.1 240.7 %all-gather.22.cloned.1.call-start = ((), (), s32[]{:S(2)}) async-start(), calls=%async_computation.12 | async-start | bytes 8650752 | tf_op jit(solution)/shard_map/all_gather | solution.py:130
  132.8 318.6 %all-gather.24.cloned.1.call-start = ((), (), s32[]{:S(2)}) async-start(), calls=%async_computation.13 | async-start | bytes 8650752 | tf_op jit(solution)/shard_map/all_gather | solution.py:131
  133.6 396.6 %all-gather.26.cloned.1.call-start = ((), (), s32[]{:S(2)}) async-start(), calls=%async_computation.14 | async-start | bytes 8650752 | tf_op jit(solution)/shard_map/all_gather | solution.py:132
  134.3 503.0 %reduce-scatter.7.cloned.1.call-start = ((), (), s32[]{:S(2)}) async-start(), calls=%async_computation.15 | async-start | bytes 2621440 | tf_op jit(solution)/shard_map/reduce_scatter | solution.py:216
  234.6 4.2 copy-start.3
  251.2 45.0 %copy-start.5 = (bf16[256,1024]{0,1:T(8,128)(2,1)}, bf16[256,1024]{0,1:T(8,128)(2,1)S(1)}, u32[]{:S(2)}) copy-start(bf16[256,1024]{0,1:T(8,128)(2,1)S(1)} %get-tuple-element.143) | copy-start | bytes 1572868
  380.4 149.8 %copy-start.12 = (bf16[1,256,1024]{2,1,0:T(8,128)(2,1)S(1)}, bf16[1,256,1024]{2,1,0:T(8,128)(2,1)}, u32[]{:S(2)}) copy-start(bf16[1,256,1024]{2,1,0:T(8,128)(2,1)} %param.27) | copy-start | bytes 1572868
  542.7 7.3 copy-start.16
  542.7 7.3 copy-start.15
  542.7 7.3 copy-start.19
  550.0 2.7 copy-start.13
  550.0 3.0 copy-start.2
  574.9 13.4 copy-start.6
  588.3 6.5 copy-start.4
  588.3 15.4 slice-start
  594.8 8.9 slice-start.1
  594.8 8.9 copy-start.11
  607.3 63.7 %reduce-scatter.9.cloned.1.call-start = ((), (), s32[]{:S(2)}) async-start(), calls=%async_computation.16 | async-start | bytes 2621440 | tf_op jit(solution)/shard_map/reduce_scatter | solution.py:219
  608.1 432.3 %reduce-scatter.11.cloned.1.call-start = ((), (), s32[]{:S(2)}) async-start(), calls=%async_computation.17 | async-start | bytes 17301504 | tf_op jit(solution)/shard_map/reduce_scatter | solution.py:234
  671.0 3.5 copy-start
  680.6 720.0 %reduce-scatter.13.cloned.1.call-start = ((), (), s32[]{:S(2)}) async-start(), calls=%async_computation.18 | async-start | bytes 17301504 | tf_op jit(solution)/shard_map/reduce_scatter | solution.py:157
  690.8 1070.0 %reduce-scatter.15.cloned.1.call-start = ((), (), s32[]{:S(2)}) async-start(), calls=%async_computation.19 | async-start | bytes 17301504 | tf_op jit(solution)/shard_map/reduce_scatter | solution.py:160
  700.5 1.0 copy-start.14
  700.6 1420.3 %reduce-scatter.17.cloned.1.call-start = ((), (), s32[]{:S(2)}) async-start(), calls=%async_computation.20 | async-start | bytes 17301504 | tf_op jit(solution)/shard_map/reduce_scatter | solution.py:163
  713.8 7.4 copy-start.7
  713.9 7.4 copy-start.9
  721.2 1.1 copy-start.8
  721.2 1.8 copy-start.10
  721.2 50.5 %copy-start.17 = (f32[256]{0:T(256)S(1)}, f32[256]{0:T(256)}, u32[]{:S(2)}) copy-start(f32[256]{0:T(256)} %get-tuple-element.129) | copy-start | bytes 3076
Sparse Core Ops, SparseCore 0:
  11.0 59.0 all-gather.9
  73.1 55.1 all-gather.15
  131.3 55.1 all-gather.13
  188.5 21.3 all-gather.11
  212.0 22.5 all-gather.17
  237.4 56.3 all-gather.19
  296.8 75.9 all-gather.21
  375.7 75.6 all-gather.23
  454.4 75.6 all-gather.25
  607.5 29.7 reduce-scatter.6
  639.8 31.1 reduce-scatter.8
  680.7 359.6 reduce-scatter.10
  1043.3 357.2 reduce-scatter.12
  1403.3 357.3 reduce-scatter.14
  1763.5 357.3 reduce-scatter.16
where the time goes:
time: 2130 us
  waiting for transfers between devices  1840 us (86%)
  matrix products  150 us (7%)
  blocking collectives  88.5 us (4%)
  local copies, waits for them, and re-layouts  24.9 us (1%)
    reduce_scatter x1, waiting for transfers between devices, local(): lax.psum_scatter(column_grad(normed_ffn, grad_up), ('seq', 'batch'), scat...  360 us
    reduce_scatter x1, waiting for transfers between devices, local(): lax.psum_scatter(column_grad(hidden, cot_rows), ('seq', 'batch'), scatter...  360 us
    reduce_scatter x1, waiting for transfers between devices, local(): lax.psum_scatter(column_grad(normed_ffn, grad_gate), ('seq', 'batch'), sc...  358 us
    reduce_scatter x1, waiting for transfers between devices, local(): lax.psum_scatter(jnp.concatenate([column_grad(normed_attn, projected_grad...  267 us
    unnamed x2, blocking collectives  88.5 us
    all_gather x1, waiting for transfers between devices, local(): lax.all_gather(w_gate, ('seq', 'batch'), axis=0, tiled=True)  76.3 us
    all_gather x1, waiting for transfers between devices, local(): lax.all_gather(w_up, ('seq', 'batch'), axis=0, tiled=True)  71 us
    all_gather x1, waiting for transfers between devices, local(): lax.all_gather(w_down, ('seq', 'batch'), axis=0, tiled=True)  71 us
  transfers between devices with their start and end apart: 15, of which 15 were waited for; matrix products, arithmetic and copies ran while one was open for 5% of the time, Pallas kernels for 0%

commit v1 on v0

--- a/solution.py
+++ b/solution.py
@@ -107,8 +107,13 @@
     key_rows_mine = project(normed_attn, attn_full[1]).astype(jnp.bfloat16)
     value_rows_mine = project(normed_attn, attn_full[2]).astype(jnp.bfloat16)
     query_heads = split_heads(query)
-    key_block = lax.all_gather(key_rows_mine, "seq", axis=0, tiled=True)
-    value_block = lax.all_gather(value_rows_mine, "seq", axis=0, tiled=True)
+    key_block, value_block = jnp.split(
+        lax.all_gather(
+            jnp.concatenate([key_rows_mine, value_rows_mine], axis=1), "seq", axis=0, tiled=True
+        ),
+        [key_rows_mine.shape[1]],
+        axis=1,
+    )
 
     def attend_compute(summed):
         gates, allowed = gating(query_heads, key_block)

time: 2130 us -> 2140 us (level)
    all_gather x1, waiting for transfers between devices: 15.1 us -> 55.7 us  [local(): lax.all_gather(w_key, ('seq', 'batch'), axis=0, tiled=True)]
    all_gather x1, waiting for transfers between devices: 54.8 us -> 15.1 us  [local(): lax.all_gather(w_value, ('seq', 'batch'), axis=0, tiled=True)]
    all_gather x2 -> x3, waiting for transfers between devices: 44.7 us -> 55.2 us  [the longest x1 31.7 us: local(): lax.all_gather(jnp.concatenate([key_rows_mine, value_rows_mine], axis=1),...]
  transfers between devices with their start and end apart: 15 -> 16, of which waited for: 15 -> 15; matrix products, arithmetic and copies ran while one was open for 5% -> 6% of each run, Pallas kernels for 0% -> 0%
where the time goes in v1:
time: 2140 us
  waiting for transfers between devices  1850 us (86%)
  matrix products  149 us (7%)
  blocking collectives  87.2 us (4%)
  local copies, waits for them, and re-layouts  29.3 us (1%)
    reduce_scatter x1, waiting for transfers between devices, local(): lax.psum_scatter(column_grad(hidden, cot_rows), ('seq', 'batch'), scatter...  360 us
    reduce_scatter x1, waiting for transfers between devices, local(): lax.psum_scatter(column_grad(normed_ffn, grad_up), ('seq', 'batch'), scat...  360 us
    reduce_scatter x1, waiting for transfers between devices, local(): lax.psum_scatter(column_grad(normed_ffn, grad_gate), ('seq', 'batch'), sc...  358 us
    reduce_scatter x1, waiting for transfers between devices, local(): lax.psum_scatter(jnp.concatenate([column_grad(normed_attn, projected_grad...  269 us
    unnamed x2, blocking collectives  87.2 us
    all_gather x1, waiting for transfers between devices, local(): lax.all_gather(w_gate, ('seq', 'batch'), axis=0, tiled=True)  76.2 us
    all_gather x1, waiting for transfers between devices, local(): lax.all_gather(w_up, ('seq', 'batch'), axis=0, tiled=True)  71 us
    all_gather x1, waiting for transfers between devices, local(): lax.all_gather(w_down, ('seq', 'batch'), axis=0, tiled=True)  71 us
  transfers between devices with their start and end apart: 16, of which 15 were waited for; matrix products, arithmetic and copies ran while one was open for 6% of the time, Pallas kernels for 0%

profile of v1, /device:TPU:0, one launch (start us, length us, event | category | flops | bytes accessed | tf_op | source)
XLA Modules:
  0.0 2139.5 jit_solution(7476101424045387695)
XLA Ops:
  7.2 0.7 all-gather.13.cloned.1.call-update
  8.0 0.7 all-gather.11.cloned.1.call-update
  8.7 0.7 all-gather.17.cloned.1.call-update
  9.5 0.8 dynamic-update-slice
  10.3 0.8 dynamic-update-slice.1
  11.2 42.1 %all-reduce.5 = (bf16[1024]{0:T(1024)(128)(2,1)S(1)}, bf16[1024]{0:T(1024)(128)(2,1)S(1)}) all-reduce(bf16[1024]{0:T(1024)(128)(2,1)S(1)} %dynamic-update-slice, bf16[1024]{0:T(1024)(128)(2,1)S(1)} %dynamic-update-slice.1), channel_id=1, replica_groups=mesh['seq'=4,'batch'=8] {'seq','batch'}, use_global_device_ids=true, to_apply=%add | all-reduce | flops 2048 | bytes 8192
  53.2 1.2 fusion.30
  55.0 15.1 all-gather.13.cloned.1.call-done
  70.1 2.5 convolution_convert_fusion.2
  72.6 55.7 %all-gather.11.cloned.1.call-done = bf16[1024,1024]{1,0:T(8,128)(2,1)} async-done(((bf16[32,1024]{1,0:T(8,128)(2,1)}), bf16[1024,1024]{1,0:T(8,128)(2,1)}) %all-gather.11.cloned.1.call-update) | async-done | bytes 2097168 | tf_op jit(solution)/shard_map/all_gather | solution.py:99
  128.3 2.3 convolution_convert_fusion.3
  130.7 1.1 pad_maximum_fusion.1
  133.1 0.7 all-gather.23.cloned.1.call-update
  133.8 0.7 all-gather.25.cloned.1.call-update
  135.3 51.2 %all-gather.17.cloned.1.call-done = bf16[1024,1024]{1,0:T(8,128)(2,1)} async-done(((bf16[32,1024]{1,0:T(8,128)(2,1)}), bf16[1024,1024]{1,0:T(8,128)(2,1)}) %all-gather.17.cloned.1.call-update) | async-done | bytes 2097168 | tf_op jit(solution)/shard_map/all_gather | solution.py:98
  186.5 2.3 convolution_convert_fusion.1
  188.9 1.0 copy.42
  190.1 31.7 %all-gather.15.cloned.1.call-done = bf16[1024,2048]{1,0:T(8,128)(2,1)} async-done(((bf16[256,2048]{1,0:T(8,128)(2,1)}), bf16[1024,2048]{1,0:T(8,128)(2,1)}) %all-gather.15.cloned.1.call-update) | async-done | bytes 4194320 | tf_op jit(solution)/shard_map/all_gather | solution.py:111
  221.9 21.1 conditional.2
  221.9 6.5 copy.43
  228.4 4.7 fusion.55
  233.4 9.5 fusion.1
  242.9 38.2 %all-gather.19.cloned.1.call-done = bf16[1024,1024]{1,0:T(8,128)(2,1)} async-done(((bf16[32,1024]{1,0:T(8,128)(2,1)}), bf16[1024,1024]{1,0:T(8,128)(2,1)}) %all-gather.19.cloned.1.call-update) | async-done | bytes 2097168 | tf_op jit(solution)/shard_map/all_gather | solution.py:101
  281.1 2.4 multiply_reduce_fusion.2
  283.7 76.2 %all-gather.21.cloned.1.call-done = bf16[1024,4096]{1,0:T(8,128)(2,1)} async-done(((bf16[32,4096]{1,0:T(8,128)(2,1)}), bf16[1024,4096]{1,0:T(8,128)(2,1)}) %all-gather.21.cloned.1.call-update) | async-done | bytes 8388624 | tf_op jit(solution)/shard_map/all_gather | solution.py:135
  359.9 7.7 fusion.57
  367.6 71.0 %all-gather.23.cloned.1.call-done = bf16[1024,4096]{1,0:T(8,128)(2,1)} async-done(((bf16[32,4096]{1,0:T(8,128)(2,1)}), bf16[1024,4096]{1,0:T(8,128)(2,1)}) %all-gather.23.cloned.1.call-update) | async-done | bytes 8388624 | tf_op jit(solution)/shard_map/all_gather | solution.py:136
  438.6 7.7 fusion.58
  446.4 71.0 %all-gather.25.cloned.1.call-done = bf16[4096,1024]{1,0:T(8,128)(2,1)} async-done(((bf16[128,1024]{1,0:T(8,128)(2,1)}), bf16[4096,1024]{1,0:T(8,128)(2,1)}) %all-gather.25.cloned.1.call-update) | async-done | bytes 8388624 | tf_op jit(solution)/shard_map/all_gather | solution.py:137
  517.3 12.5 multiply_convert_fusion
  529.8 7.3 fusion.59
  537.2 2.6 multiply_reduce_fusion
  540.2 1.5 convolution_convert_fusion
  541.8 23.5 %all-gather.29.cloned.1.call-done = bf16[1024,1024]{1,0:T(8,128)(2,1)} async-done(((bf16[256,1024]{1,0:T(8,128)(2,1)}), bf16[1024,1024]{1,0:T(8,128)(2,1)}) %all-gather.29.cloned.1.call-update) | async-done | bytes 2097168 | tf_op jit(solution)/shard_map/all_gather | solution.py:186
  565.3 52.8 %conditional.3 = (bf16[1024,1024]{0,1:T(8,128)(2,1)}, bf16[1024,1024]{0,1:T(8,128)(2,1)}, bf16[256,1024]{0,1:T(8,128)(2,1)}) conditional(s32[]{:T(128)} %convert_element_type.97, () %tuple.28, (s32[4]{0:T(128)S(1)}, s32[1,4]{1,0:T(1,128)S(1)}, s32[256]{0:T(256)S(1)}, bf16[256,1024]{1,0:T(8,128)(2,1)}, bf16[1024,1024]{1,0:T(8,128)(2,1)}, ...), branch_computations={%region_6.7_spmd, %region_7.9_spmd} | conditional | flops 2733668352 | bytes 134499488 | solution.py:217
  565.3 4.0 copy.46
  569.2 9.6 add_divide_fusion
  578.8 2.0 copy.44
  580.9 4.3 copy.45
  585.6 13.4 select_convert_fusion.2
  598.9 6.6 convolution_multiply_fusion
  605.6 9.0 fusion.11
  614.5 3.6 fusion.14
  618.8 3.7 fusion.45
  622.5 27.0 %reduce-scatter.7.cloned.1.call-done = bf16[256,1024]{0,1:T(8,128)(2,1)} async-done(((bf16[1024,1024]{0,1:T(8,128)(2,1)}), bf16[256,1024]{0,1:T(8,128)(2,1)}) %reduce-scatter.7.cloned.1.call-update) | async-done | bytes 524304 | tf_op jit(solution)/shard_map/reduce_scatter | solution.py:221
  649.5 33.6 %reduce-scatter.9.cloned.1.call-done = bf16[256,1024]{0,1:T(8,128)(2,1)} async-done(((bf16[1024,1024]{0,1:T(8,128)(2,1)}), bf16[256,1024]{0,1:T(8,128)(2,1)}) %reduce-scatter.9.cloned.1.call-update) | async-done | bytes 524304 | tf_op jit(solution)/shard_map/reduce_scatter | solution.py:224
  683.1 3.5 fusion.22
  686.6 6.1 pad_maximum_fusion
  692.9 9.9 fusion.61
  702.9 9.7 fusion.62
  712.7 1.0 copy-done.12
  713.7 9.7 fusion.41
  723.4 2.5 fusion.60
  726.0 7.3 fusion.29
  733.4 0.8 convolution_add_fusion.1
  734.4 0.8 copy-done.7
  735.1 1.1 fusion.40
  736.2 45.2 %all-reduce.4 = (f32[1024]{0:T(1024)S(1)}, f32[1024]{0:T(1024)S(1)}) all-reduce(f32[1024]{0:T(1024)S(1)} %get-tuple-element.112, f32[1024]{0:T(1024)S(1)} %get-tuple-element.110), channel_id=5, replica_groups=mesh['seq'=4,'batch'=8] {'seq','batch'}, use_global_device_ids=true, to_apply=%region_14.15.clone | all-reduce | flops 2048 | bytes 16384
  782.5 1.3 fusion.37
  783.8 268.6 %reduce-scatter.11.cloned.1.call-done = f32[32,4096]{1,0:T(8,128)} async-done(((f32[1024,4096]{1,0:T(8,128)}), f32[32,4096]{1,0:T(8,128)}) %reduce-scatter.11.cloned.1.call-update) | async-done | bytes 524304 | tf_op jit(solution)/shard_map/reduce_scatter | solution.py:239
  1052.5 1.9 fusion.56
  1054.4 358.2 %reduce-scatter.13.cloned.1.call-done = f32[32,4096]{1,0:T(8,128)} async-done(((f32[1024,4096]{1,0:T(8,128)}), f32[32,4096]{1,0:T(8,128)}) %reduce-scatter.13.cloned.1.call-update) | async-done | bytes 524304 | tf_op jit(solution)/shard_map/reduce_scatter | solution.py:162
  1412.6 360.1 %reduce-scatter.15.cloned.1.call-done = f32[32,4096]{1,0:T(8,128)} async-done(((f32[1024,4096]{1,0:T(8,128)}), f32[32,4096]{1,0:T(8,128)}) %reduce-scatter.15.cloned.1.call-update) | async-done | bytes 524304 | tf_op jit(solution)/shard_map/reduce_scatter | solution.py:165
  1772.7 360.1 %reduce-scatter.17.cloned.1.call-done = f32[128,1024]{1,0:T(8,128)} async-done(((f32[4096,1024]{1,0:T(8,128)}), f32[128,1024]{1,0:T(8,128)}) %reduce-scatter.17.cloned.1.call-update) | async-done | bytes 524304 | tf_op jit(solution)/shard_map/reduce_scatter | solution.py:168
  (94 shorter events, 6.7 us)
Async XLA Ops:
  7.2 121.1 %copy-start.1 = (bf16[1,256,1024]{2,1,0:T(8,128)(2,1)S(1)}, bf16[1,256,1024]{2,1,0:T(8,128)(2,1)}, u32[]{:S(2)}) copy-start(bf16[1,256,1024]{2,1,0:T(8,128)(2,1)} %param.16) | copy-start | bytes 1572868
  7.2 62.9 %all-gather.13.cloned.1.call-start = ((), (), s32[]{:S(2)}) async-start(), calls=%async_computation.7 | async-start | bytes 2162688 | tf_op jit(solution)/shard_map/all_gather | solution.py:100
  7.9 120.4 %all-gather.11.cloned.1.call-start = ((), (), s32[]{:S(2)}) async-start(), calls=%async_computation.6 | async-start | bytes 2162688 | tf_op jit(solution)/shard_map/all_gather | solution.py:99
  8.7 177.9 %all-gather.17.cloned.1.call-start = ((), (), s32[]{:S(2)}) async-start(), calls=%async_computation.9 | async-start | bytes 2162688 | tf_op jit(solution)/shard_map/all_gather | solution.py:98
  9.4 212.5 %all-gather.15.cloned.1.call-start = ((), (), s32[]{:S(2)}) async-start(), calls=%async_computation.8 | async-start | bytes 5242880 | tf_op jit(solution)/shard_map/all_gather | solution.py:111
  72.6 61.9 %copy-start.13 = (bf16[256,1024]{1,0:T(8,128)(2,1)}, bf16[256,1024]{1,0:T(8,128)(2,1)S(1)}, u32[]{:S(2)}) copy-start(bf16[256,1024]{1,0:T(8,128)(2,1)S(1)} %convolution_convert_fusion.2) | copy-start | bytes 1572868
  130.7 59.2 %copy-start.14 = (bf16[256,1024]{1,0:T(8,128)(2,1)}, bf16[256,1024]{1,0:T(8,128)(2,1)S(1)}, u32[]{:S(2)}) copy-start(bf16[256,1024]{1,0:T(8,128)(2,1)S(1)} %convolution_convert_fusion.3) | copy-start | bytes 1572868
  131.8 90.1 %copy-start.18 = (s32[1,4]{1,0:T(1,128)S(1)}, s32[1,4]{1,0:T(1,128)}, u32[]{:S(2)}) copy-start(s32[1,4]{1,0:T(1,128)} %param.26) | copy-start | bytes 52
  131.8 149.3 %all-gather.19.cloned.1.call-start = ((), (), s32[]{:S(2)}) async-start(), calls=%async_computation.10 | async-start | bytes 2162688 | tf_op jit(solution)/shard_map/all_gather | solution.py:101
  132.4 227.5 %all-gather.21.cloned.1.call-start = ((), (), s32[]{:S(2)}) async-start(), calls=%async_computation.11 | async-start | bytes 8650752 | tf_op jit(solution)/shard_map/all_gather | solution.py:135
  133.0 305.6 %all-gather.23.cloned.1.call-start = ((), (), s32[]{:S(2)}) async-start(), calls=%async_computation.12 | async-start | bytes 8650752 | tf_op jit(solution)/shard_map/all_gather | solution.py:136
  133.8 383.6 %all-gather.25.cloned.1.call-start = ((), (), s32[]{:S(2)}) async-start(), calls=%async_computation.13 | async-start | bytes 8650752 | tf_op jit(solution)/shard_map/all_gather | solution.py:137
  134.5 407.3 %all-gather.27.cloned.1.call-start = ((), (), s32[]{:S(2)}) async-start(), calls=%async_computation.14 | async-start | bytes 2621440 | tf_op jit(solution)/shard_map/all_gather | solution.py:187
  135.2 430.0 %all-gather.29.cloned.1.call-start = ((), (), s32[]{:S(2)}) async-start(), calls=%async_computation.15 | async-start | bytes 2621440 | tf_op jit(solution)/shard_map/all_gather | solution.py:186
  189.9 459.6 %reduce-scatter.7.cloned.1.call-start = ((), (), s32[]{:S(2)}) async-start(), calls=%async_computation.16 | async-start | bytes 2621440 | tf_op jit(solution)/shard_map/reduce_scatter | solution.py:221
  242.9 124.7 %copy-start.4 = (bf16[256,1024]{0,1:T(8,128)(2,1)}, bf16[256,1024]{0,1:T(8,128)(2,1)S(1)}, u32[]{:S(2)}) copy-start(bf16[256,1024]{0,1:T(8,128)(2,1)S(1)} %get-tuple-element.141) | copy-start | bytes 1572868
  367.6 149.8 %copy-start.10 = (bf16[1,256,1024]{2,1,0:T(8,128)(2,1)S(1)}, bf16[1,256,1024]{2,1,0:T(8,128)(2,1)}, u32[]{:S(2)}) copy-start(bf16[1,256,1024]{2,1,0:T(8,128)(2,1)} %param.27) | copy-start | bytes 1572868
  529.8 7.3 copy-start.16
  529.8 7.4 copy-start.15
  529.8 7.4 copy-start.19
  537.2 2.7 copy-start.11
  537.2 3.0 copy-start.2
  598.9 6.6 copy-start.3
  598.9 15.6 slice-start
  605.6 9.0 slice-start.1
  605.6 9.0 copy-start.9
  618.1 64.9 %reduce-scatter.9.cloned.1.call-start = ((), (), s32[]{:S(2)}) async-start(), calls=%async_computation.17 | async-start | bytes 2621440 | tf_op jit(solution)/shard_map/reduce_scatter | solution.py:224
  618.7 433.8 %reduce-scatter.11.cloned.1.call-start = ((), (), s32[]{:S(2)}) async-start(), calls=%async_computation.18 | async-start | bytes 17301504 | tf_op jit(solution)/shard_map/reduce_scatter | solution.py:239
  683.1 3.5 copy-start
  692.7 719.9 %reduce-scatter.13.cloned.1.call-start = ((), (), s32[]{:S(2)}) async-start(), calls=%async_computation.19 | async-start | bytes 17301504 | tf_op jit(solution)/shard_map/reduce_scatter | solution.py:162
  702.9 1069.8 %reduce-scatter.15.cloned.1.call-start = ((), (), s32[]{:S(2)}) async-start(), calls=%async_computation.20 | async-start | bytes 17301504 | tf_op jit(solution)/shard_map/reduce_scatter | solution.py:165
  712.6 1.0 copy-start.12
  712.7 1420.1 %reduce-scatter.17.cloned.1.call-start = ((), (), s32[]{:S(2)}) async-start(), calls=%async_computation.21 | async-start | bytes 17301504 | tf_op jit(solution)/shard_map/reduce_scatter | solution.py:168
  726.0 7.4 copy-start.5
  726.0 7.4 copy-start.8
  733.3 1.1 copy-start.6
  733.3 1.8 copy-start.7
  733.3 49.2 %copy-start.17 = (f32[256]{0:T(256)S(1)}, f32[256]{0:T(256)}, u32[]{:S(2)}) copy-start(f32[256]{0:T(256)} %get-tuple-element.127) | copy-start | bytes 3076
Sparse Core Ops, SparseCore 0:
  11.0 59.0 all-gather.12
  73.1 55.2 all-gather.10
  131.3 55.2 all-gather.16
  188.5 33.2 all-gather.14
  224.7 56.3 all-gather.18
  283.9 75.9 all-gather.20
  362.9 75.6 all-gather.22
  441.6 75.6 all-gather.24
  519.5 21.1 all-gather.26
  542.7 22.5 all-gather.28
  618.3 31.1 reduce-scatter.6
  651.9 31.1 reduce-scatter.8
  692.8 359.6 reduce-scatter.10
  1055.2 357.3 reduce-scatter.12
  1415.3 357.3 reduce-scatter.14
  1775.4 357.3 reduce-scatter.16
